TPU v7x, 256 devices: a whole 4x4x8 slice. The times are simulated.
256 devices in a mesh: feature: 4 (over x), kvhead: 8 (over y, core), seq: 8 (over z).
Axes of the slice: x: 4, y: 4, z: 8, core: 2. Of those that a mesh axis runs over, the one named last changes fastest.
Arguments:
- queries: float32 [2048, 40, 128], P('seq', 'kvhead'), may hold values from -6 to 6
- keys: float32 [2048, 8, 128], P('seq', 'kvhead'), may hold values from -6 to 6
- values: float32 [2048, 8, 128], P('seq', 'kvhead'), may hold values from -6 to 6
- w_out: float32 [5120, 5120], P('kvhead', ('feature', 'seq')), may hold values from -0.078125 to 0.078125
Outputs:
- projected: float32 [2048, 5120], P(('seq', 'feature'), 'kvhead')
All inputs are finite; a program needn't handle non-finite values.
Results may differ from a plain program's by a relative error of at most 0.0003.
Values sent between devices are 32-bit elements; how exact they have to be, the bound alone decides.
A program may use at most 128 MiB of HBM per device.

v0:
```python
import math
import jax
import jax.numpy as jnp
import numpy as np
from jax import lax
from jax.sharding import PartitionSpec as P


def from_everyone(x, axis):
    copies = jnp.broadcast_to(x, (lax.axis_size(axis), *x.shape))
    return lax.all_to_all(copies, axis, split_axis=0, concat_axis=0, tiled=True)


def of_everyone(x, axis):
    everything = from_everyone(x, axis)
    return jnp.sum(everything, axis=0)


def in_blocks(x, dim, count):
    before, after = (x.shape[:dim], x.shape[dim + 1 :])
    return jnp.moveaxis(x.reshape(*before, count, -1, *after), dim, 0)


def summed_on_arrival(x, axis, dim):
    count = lax.axis_size(axis)
    blocks = lax.all_to_all(in_blocks(x, dim, count), axis, 0, 0, tiled=True)
    return jnp.sum(blocks, axis=0)


def expand(vectors, select_first, select_second, factor):
    highest = lax.Precision.HIGHEST
    left = jnp.einsum("...d,df->...f", vectors, select_first, precision=highest)
    right = jnp.einsum("...d,df->...f", vectors, select_second, precision=highest)
    return left * right * factor


def local(queries, keys, values, w_out):
    rows, local_heads, head_size = queries.shape
    kv_local = keys.shape[1]
    group = local_heads // kv_local
    parts = lax.axis_size("feature")
    position = lax.axis_index("feature")
    width = head_size * (head_size + 1) // 2 // parts
    upper_i, upper_j = np.triu_indices(head_size)
    factor_table = np.where(upper_i == upper_j, 1.0, math.sqrt(2.0)).astype(np.float32)
    first = lax.dynamic_slice_in_dim(jnp.asarray(upper_i.astype(np.int32)), position * width, width)
    second = lax.dynamic_slice_in_dim(
        jnp.asarray(upper_j.astype(np.int32)), position * width, width
    )
    factor = lax.dynamic_slice_in_dim(jnp.asarray(factor_table), position * width, width)
    entries = jnp.arange(head_size, dtype=jnp.int32)
    select_first = (entries[:, None] == first[None, :]).astype(jnp.float32)
    select_second = (entries[:, None] == second[None, :]).astype(jnp.float32)
    quarter = rows // parts
    scaled = (queries * head_size ** (-0.5)).reshape(rows, kv_local, group, head_size)
    highest = lax.Precision.HIGHEST
    block_states = []
    block_norms = []
    for block in range(parts):
        key_part = keys[block * quarter : (block + 1) * quarter]
        lifted = expand(key_part, select_first, select_second, factor)
        block_states.append(
            jnp.einsum(
                "tkf,tkd->kfd",
                lifted,
                values[block * quarter : (block + 1) * quarter],
                precision=highest,
            )
        )
        block_norms.append(jnp.sum(lifted, axis=0))
    total_state = sum(block_states)
    total_norm = sum(block_norms)
    own_index = lax.axis_index("seq")
    empty = (jnp.zeros_like(total_state), jnp.zeros_like(total_norm))
    pieces = (
        lax.all_gather(total_state[None], "seq", axis=0, tiled=True),
        lax.all_gather(total_norm[None], "seq", axis=0, tiled=True),
    )
    count = pieces[0].shape[0]
    keep = (jnp.arange(count, dtype=jnp.int32) < own_index).astype(jnp.float32)
    prior_state = empty[0] + jnp.einsum("n,nkfd->kfd", keep, pieces[0], precision=highest)
    prior_norm = empty[1] + jnp.einsum("n,nkf->kf", keep, pieces[1], precision=highest)
    running_state = prior_state
    running_norm = prior_norm
    numerators = []
    denominators = []
    for block in range(parts):
        lifted_query = expand(
            scaled[block * quarter : (block + 1) * quarter], select_first, select_second, factor
        )
        numerators.append(
            jnp.einsum("tkgf,kfd->tkgd", lifted_query, running_state, precision=highest)
        )
        denominators.append(
            jnp.einsum("tkgf,kf->tkg", lifted_query, running_norm, precision=highest)
        )
        running_state = running_state + block_states[block]
        running_norm = running_norm + block_norms[block]
    numerator = jnp.concatenate(numerators, axis=0)
    denominator = jnp.concatenate(denominators, axis=0)
    own_start = position * quarter
    own_query = lax.dynamic_slice_in_dim(scaled, own_start, quarter, 0)
    own_key = lax.dynamic_slice_in_dim(keys, own_start, quarter, 0)
    own_value = lax.dynamic_slice_in_dim(values, own_start, quarter, 0)
    scores = jnp.einsum("tkgd,skd->kgts", own_query, own_key, precision=highest)
    causal = jnp.tril(jnp.ones((quarter, quarter), jnp.bool_))
    squared = jnp.where(causal[None, None], scores * scores, jnp.float32(0.0))
    inner_numerator = jnp.einsum("kgts,skd->tkgd", squared, own_value, precision=highest)
    inner_denominator = jnp.transpose(jnp.sum(squared, axis=-1), (2, 0, 1))
    numerator = lax.dynamic_update_slice_in_dim(
        numerator,
        lax.dynamic_slice_in_dim(numerator, own_start, quarter, 0) + inner_numerator,
        own_start,
        0,
    )
    denominator = lax.dynamic_update_slice_in_dim(
        denominator,
        lax.dynamic_slice_in_dim(denominator, own_start, quarter, 0) + inner_denominator,
        own_start,
        0,
    )
    whole_numerator, whole_denominator = (
        of_everyone(numerator, "feature"),
        of_everyone(denominator, "feature"),
    )
    share_numerator = lax.dynamic_slice_in_dim(whole_numerator, own_start, quarter, 0)
    share_denominator = lax.dynamic_slice_in_dim(whole_denominator, own_start, quarter, 0)
    attended = (share_numerator / (share_denominator[..., None] + 1.0)).reshape(
        quarter, local_heads * head_size
    )
    partial_out = jnp.dot(
        attended,
        lax.all_gather(w_out, ("feature", "seq"), axis=1, tiled=True),
        precision=highest,
        preferred_element_type=jnp.float32,
    )
    return summed_on_arrival(partial_out, "kvhead", 1)


def solution(mesh):
    in_specs = (
        P("seq", "kvhead", None),
        P("seq", "kvhead", None),
        P("seq", "kvhead", None),
        P("kvhead", ("feature", "seq")),
    )
    out_specs = P(("seq", "feature"), "kvhead")
    return jax.shard_map(local, mesh=mesh, in_specs=in_specs, out_specs=out_specs, check_vma=False)
```

profile of v0, /device:TPU:1, one launch (start us, length us, event | category | flops | bytes accessed | tf_op | source)
XLA Modules:
  0.0 359.7 jit_solution(14535412155245520975)
XLA Ops:
  6.5 0.8 dynamic_slice.24
  7.3 0.8 dynamic_slice.26
  8.1 0.8 dynamic_slice.25
  8.9 0.8 constant_dynamic-slice_fusion.1
  9.8 0.9 fusion.26
  10.6 0.9 fusion.27
  11.5 0.9 fusion.82
  12.3 0.9 fusion.83
  13.2 0.9 fusion.25
  14.1 1.7 fusion.84
  15.7 0.9 fusion.28
  16.6 1.7 fusion.85
  18.2 0.6 dynamic-slice.12
  19.7 0.6 copy-done.9
  20.6 1.9 fusion.90
  22.4 1.9 fusion.89
  24.3 1.9 fusion.88
  26.2 2.9 convolution_add_fusion
  29.9 1.1 broadcast_multiply_fusion
  31.6 1.4 fusion.29
  33.0 1.4 fusion.31
  34.4 1.4 fusion.33
  35.8 1.4 fusion.35
  37.1 3.1 fusion.2
  40.2 3.1 fusion.3
  43.4 3.1 fusion.4
  46.5 3.0 fusion.5
  49.5 40.5 %all-reduce.3.cloned.1.call-done = f32[16512]{0:T(1024)} async-done(((f32[16512]{0:T(1024)}), f32[16512]{0:T(1024)}) %all-reduce.3.cloned.1.call-update) | async-done | bytes 66064
  90.1 1.0 reshape.274
  91.3 5.7 %convolution_bitcast_fusion.6 = f32[64,1,5]{0,1,2:T(1,128)S(1)} fusion(f32[2064,1,1]{0,1,2:T(1,128)S(1)} %reshape.303, f32[64,5,2064]{2,0,1:T(8,128)} %fusion.2), kind=kOutput, calls=%fused_computation.31 | convolution fusion | flops 7925760 | bytes 2651456 | tf_op jit(solution)/shard_map/tkgf,kf->tkg/dot_general | solution.py:95
  97.0 3.3 convolution_bitcast_fusion.7
  100.3 3.3 convolution_bitcast_fusion.8
  103.6 3.3 convolution_bitcast_fusion.9
  107.4 0.6 broadcast_in_dim.20
  108.0 4.1 %all-to-all-start.1 = ((f32[4,256,1,5]{1,2,3,0:T(1,128)}), f32[4,256,1,5]{1,2,3,0:T(1,128)S(1)}, u32[]{:S(2)}, u32[]{:S(2)}) async-start(f32[4,256,1,5]{1,2,3,0:T(1,128)} %broadcast_in_dim.20), calls=%async_computation.1 | async-start | bytes 40960 | tf_op jit(solution)/shard_map/all_to_all | solution.py:11
  112.1 77.6 %all-gather.7.cloned.1.call-done = f32[16512,128]{1,0:T(8,128)} async-done(((f32[2064,128]{1,0:T(8,128)}), f32[16512,128]{1,0:T(8,128)}) %all-gather.7.cloned.1.call-update) | async-done | bytes 8454160 | tf_op jit(solution)/shard_map/all_gather | solution.py:76
  189.7 9.6 %fusion = f32[1,2064,128]{2,0,1:T(1,128)S(1)} fusion(f32[8,2064,128]{2,1,0:T(8,128)} %bitcast.154, s32[]{:T(128)S(6)} %axis_index.22), kind=kOutput, calls=%fused_computation | convolution fusion | flops 25362440 | bytes 9510916 | tf_op jit(solution)/shard_map/n,nkfd->kfd/dot_general | solution.py:81
  199.3 2.4 convolution_bitcast_fusion.5
  201.8 2.4 convolution_bitcast_fusion.4
  204.2 2.7 convolution_bitcast_fusion.3
  206.9 2.5 convolution_bitcast_fusion.2
  210.0 1.7 broadcast_in_dim.19
  211.8 4.0 %all-to-all-start = ((f32[4,256,1,5,128]{4,1,3,2,0:T(8,128)}), f32[4,256,1,5,128]{4,1,3,2,0:T(8,128)S(1)}, u32[]{:S(2)}, u32[]{:S(2)}) async-start(f32[4,256,1,5,128]{4,1,3,2,0:T(8,128)} %broadcast_in_dim.19), calls=%async_computation | async-start | bytes 5242880 | tf_op jit(solution)/shard_map/all_to_all | solution.py:11
  215.8 32.7 %all-to-all-done = f32[4,256,1,5,128]{4,1,3,2,0:T(8,128)S(1)} async-done(((f32[4,256,1,5,128]{4,1,3,2,0:T(8,128)}), f32[4,256,1,5,128]{4,1,3,2,0:T(8,128)S(1)}, u32[]{:S(2)}, u32[]{:S(2)}) %all-to-all-start) | async-done | bytes 2621472 | tf_op jit(solution)/shard_map/all_to_all | solution.py:11
  249.1 64.6 %all-gather.5.cloned.1.call-done = f32[640,5120]{0,1:T(8,128)} async-done(((f32[640,160]{0,1:T(8,128)}), f32[640,5120]{0,1:T(8,128)}) %all-gather.5.cloned.1.call-update) | async-done | bytes 13107216 | tf_op jit(solution)/shard_map/all_gather | solution.py:133
  313.6 15.7 %convolution_bitcast_fusion = f32[8,64,640]{2,1,0:T(8,128)S(1)} fusion(f32[64,640,1]{1,0,2:T(8,128)S(1)} %reshape.305, f32[8,640,640]{2,1,0:T(8,128)} %bitcast.153), kind=kOutput, calls=%fused_computation.19 | convolution fusion | flops 2516582400 | bytes 14581760 | tf_op jit(solution)/shard_map/dot_general | solution.py:131
  329.4 22.8 %all_to_all.15 = f32[8,64,640]{2,1,0:T(8,128)S(1)} all-to-all(f32[8,64,640]{2,1,0:T(8,128)S(1)} %convolution_bitcast_fusion), channel_id=1, replica_groups=mesh['feature'=4,'kvhead'=8,'seq'=8] {'kvhead'}, dimensions={0} | all-to-all | bytes 2621440 | tf_op jit(solution)/shard_map/all_to_all | solution.py:26
  352.2 0.7 reduce_sum.82
  (53 shorter events, 3.5 us)
Async XLA Ops:
  6.5 83.5 %all-reduce.3.cloned.1.call-start = ((), (), s32[]{:S(2)}) async-start(), calls=%async_computation.5 | async-start | bytes 139264
  15.7 2.5 copy-start.11
  15.7 4.8 %copy-start.10 = (f32[256,1,128]{2,1,0:T(1,128)S(1)}, f32[256,1,128]{2,1,0:T(1,128)}, u32[]{:S(2)}) copy-start(f32[256,1,128]{2,1,0:T(1,128)} %param.9) | copy-start | bytes 393220
  19.6 0.6 copy-start.9
  20.3 169.4 %all-gather.7.cloned.1.call-start = ((), (), s32[]{:S(2)}) async-start(), calls=%async_computation.4 | async-start | bytes 9510912 | tf_op jit(solution)/shard_map/all_gather | solution.py:76
  22.4 1.9 copy-start.8
  24.3 1.9 copy-start.7
  29.2 284.5 %all-gather.5.cloned.1.call-start = ((), (), s32[]{:S(2)}) async-start(), calls=%async_computation.3 | async-start | bytes 13516800 | tf_op jit(solution)/shard_map/all_gather | solution.py:133
  91.3 5.7 %copy-start.1 = (f32[64,5,2064]{2,0,1:T(8,128)S(1)}, f32[64,5,2064]{2,0,1:T(8,128)}, u32[]{:S(2)}) copy-start(f32[64,5,2064]{2,0,1:T(8,128)} %fusion.3) | copy-start | bytes 7925764
  96.9 3.3 copy-start.3
  100.3 3.3 copy-start.5
  108.0 102.0 %all-to-all-start.1 = ((f32[4,256,1,5]{1,2,3,0:T(1,128)}), f32[4,256,1,5]{1,2,3,0:T(1,128)S(1)}, u32[]{:S(2)}, u32[]{:S(2)}) async-start(f32[4,256,1,5]{1,2,3,0:T(1,128)} %broadcast_in_dim.20), calls=%async_computation.1 | async-start | bytes 40960 | tf_op jit(solution)/shard_map/all_to_all | solution.py:11
  189.7 9.6 %copy-start.6 = (f32[64,5,2064]{2,0,1:T(8,128)S(1)}, f32[64,5,2064]{2,0,1:T(8,128)}, u32[]{:S(2)}) copy-start(f32[64,5,2064]{2,0,1:T(8,128)} %fusion.5) | copy-start | bytes 7925764
  199.3 2.4 copy-start.4
  201.7 2.4 copy-start.2
  204.2 2.7 copy-start
  211.8 36.8 %all-to-all-start = ((f32[4,256,1,5,128]{4,1,3,2,0:T(8,128)}), f32[4,256,1,5,128]{4,1,3,2,0:T(8,128)S(1)}, u32[]{:S(2)}, u32[]{:S(2)}) async-start(f32[4,256,1,5,128]{4,1,3,2,0:T(8,128)} %broadcast_in_dim.19), calls=%async_computation | async-start | bytes 5242880 | tf_op jit(solution)/shard_map/all_to_all | solution.py:11
Sparse Core Ops, SparseCore 0:
  20.4 69.5 all-reduce.2
  91.8 97.8 all-gather.6
  192.3 121.2 all-gather.4
where the time goes:
time: 365 us; the launch traced here: 360 us
  waiting for transfers between devices  216 us (59%)
  matrix products  87.1 us (24%)
  blocking collectives  22.8 us (6%)
  between operations  14.4 us (4%)
  starting transfers between devices  8.51 us (2%)
  local copies, waits for them, and re-layouts  8.29 us (2%)
    all_gather x1, waiting for transfers between devices, local(): lax.all_gather(total_state[None], 'seq', axis=0, tiled=True)  77.6 us
    all_gather x1, waiting for transfers between devices, local(): lax.all_gather(w_out, ('feature', 'seq'), axis=1, tiled=True)  64.6 us
    unnamed x4, waiting for transfers between devices  41 us
    all_to_all x2, waiting for transfers between devices, from_everyone(): return lax.all_to_all(copies, axis, split_axis=0, concat_axis=0, tiled=True)  32.7 us
    all_to_all x1, blocking collectives, summed_on_arrival(): blocks = lax.all_to_all(in_blocks(x, dim, count), axis, 0, 0, tiled=True)  22.8 us
    dot_general x8, matrix products, expand(): jnp.einsum('...d,df->...f', vectors, select_second, precision=highest)  17.4 us
    dot_general x1, matrix products, local(): jnp.dot(attended, lax.all_gather(w_out, ('feature', 'seq'), axis=1, tiled...  15.7 us
    dot_general x4, matrix products, local(): jnp.einsum('tkgf,kf->tkg', lifted_query, running_norm, precision=highest)  15.7 us
  transfers between devices with their start and end apart: 5, of which 4 were waited for; matrix products, arithmetic and copies ran while one was open for 19% of the time, Pallas kernels for 0%

commit v1 on v0

--- a/solution.py
+++ b/solution.py
@@ -130,7 +130,12 @@
     )
     partial_out = jnp.dot(
         attended,
-        lax.all_gather(w_out, ("feature", "seq"), axis=1, tiled=True),
+        jnp.concatenate(
+            lax.all_to_all(
+                jnp.stack([w_out] * lax.axis_size(("feature", "seq"))), ("feature", "seq"), 0, 0
+            ),
+            axis=1,
+        ),
         precision=highest,
         preferred_element_type=jnp.float32,
     )

time: 365 us -> 617 us (1.69)
  the two profiles are of different devices: /device:TPU:1 before, /device:TPU:166 now
where the time goes in v1:
time: 617 us; the launch traced here: 612 us
  waiting for transfers between devices  423 us (69%)
  matrix products  87.3 us (14%)
  blocking collectives  57.3 us (9%)
  between operations  14.7 us (2%)
  starting transfers between devices  13.7 us (2%)
  local copies, waits for them, and re-layouts  13 us (2%)
    all_to_all x1, waiting for transfers between devices, local(): lax.all_to_all(jnp.stack([w_out] * lax.axis_size(('feature', 'seq'))), ('...  310 us
    all_gather x1, waiting for transfers between devices, local(): lax.all_gather(total_state[None], 'seq', axis=0, tiled=True)  73.3 us
    unnamed x3, waiting for transfers between devices  40.1 us
    all_to_all x1, blocking collectives, from_everyone(): return lax.all_to_all(copies, axis, split_axis=0, concat_axis=0, tiled=True)  34.4 us
    all_to_all x1, blocking collectives, summed_on_arrival(): blocks = lax.all_to_all(in_blocks(x, dim, count), axis, 0, 0, tiled=True)  22.9 us
    dot_general x8, matrix products, expand(): jnp.einsum('...d,df->...f', vectors, select_second, precision=highest)  17.5 us
    dot_general x1, matrix products, local(): jnp.dot(attended, jnp.concatenate(lax.all_to_all(jnp.stack([w_out] * lax....  15.7 us
    dot_general x4, matrix products, local(): jnp.einsum('tkgf,kf->tkg', lifted_query, running_norm, precision=highest)  15.5 us
  transfers between devices with their start and end apart: 4, of which 3 were waited for; matrix products, arithmetic and copies ran while one was open for 11% of the time, Pallas kernels for 0%

profile of v1, /device:TPU:166, one launch (start us, length us, event | category | flops | bytes accessed | tf_op | source)
XLA Modules:
  0.0 611.8 jit_solution(4481353330775592442)
XLA Ops:
  6.5 0.8 dynamic_slice.24
  7.3 0.8 dynamic_slice.25
  8.1 0.8 dynamic_slice.26
  8.9 0.8 constant_dynamic-slice_fusion.1
  9.7 0.9 fusion.26
  10.6 0.9 fusion.27
  11.5 0.9 fusion.82
  12.3 0.9 fusion.83
  13.2 0.9 fusion.28
  14.0 1.7 fusion.85
  15.7 0.9 fusion.25
  16.6 1.7 fusion.84
  18.2 0.6 dynamic-slice.12
  19.6 0.6 copy-done.10
  20.5 1.9 fusion.90
  22.4 1.9 fusion.89
  24.3 1.9 fusion.88
  26.2 2.9 convolution_add_fusion
  29.1 1.1 broadcast_multiply_fusion
  30.8 1.4 fusion.29
  32.2 1.4 fusion.31
  33.6 1.4 fusion.33
  35.0 1.8 fusion.35
  36.8 3.1 fusion.2
  39.9 3.2 fusion.3
  43.1 3.1 fusion.4
  46.2 3.1 fusion.5
  49.2 40.1 %all-reduce.3.cloned.1.call-done = f32[16512]{0:T(1024)} async-done(((f32[16512]{0:T(1024)}), f32[16512]{0:T(1024)}) %all-reduce.3.cloned.1.call-update) | async-done | bytes 66064
  89.4 1.0 reshape.282
  90.6 5.3 convolution_bitcast_fusion.6
  95.9 3.3 convolution_bitcast_fusion.7
  99.2 3.5 convolution_bitcast_fusion.8
  102.7 3.3 convolution_bitcast_fusion.9
  106.5 0.6 broadcast_in_dim.20
  107.1 4.7 all-to-all-start.1
  111.8 73.3 %all-gather.4.cloned.1.call-done = f32[16512,128]{1,0:T(8,128)} async-done(((f32[2064,128]{1,0:T(8,128)}), f32[16512,128]{1,0:T(8,128)}) %all-gather.4.cloned.1.call-update) | async-done | bytes 8454160 | tf_op jit(solution)/shard_map/all_gather | solution.py:76
  185.1 9.6 %fusion = f32[1,2064,128]{2,0,1:T(1,128)S(1)} fusion(f32[8,2064,128]{2,1,0:T(8,128)} %bitcast.157, s32[]{:T(128)S(6)} %axis_index.22), kind=kOutput, calls=%fused_computation | convolution fusion | flops 25362440 | bytes 9510916 | tf_op jit(solution)/shard_map/n,nkfd->kfd/dot_general | solution.py:81
  194.7 2.5 convolution_bitcast_fusion.2
  197.3 2.5 convolution_bitcast_fusion.3
  199.8 2.6 convolution_bitcast_fusion.4
  202.4 2.4 convolution_bitcast_fusion.5
  205.7 34.4 %all_to_all.20 = f32[4,256,1,5,128]{4,1,3,2,0:T(8,128)S(1)} all-to-all(f32[4,256,1,5,128]{4,1,3,2,0:T(8,128)S(1)} %broadcast_in_dim.19), channel_id=1, replica_groups=mesh['feature'=4,'kvhead'=8,'seq'=8] {'feature'}, dimensions={0} | all-to-all | bytes 5242880 | tf_op jit(solution)/shard_map/all_to_all | solution.py:11
  240.1 6.2 %stack.2 = f32[32,640,160]{1,2,0:T(8,128)} broadcast(f32[640,160]{0,1:T(8,128)S(1)} %copy-done.9), dimensions={1,2} | broadcast | bytes 13516800 | tf_op jit(solution)/shard_map/stack | solution.py:135
  246.3 8.8 %all-to-all-start.2 = ((f32[32,640,160]{1,2,0:T(8,128)}), f32[32,640,160]{1,2,0:T(8,128)}, u32[]{:S(2)}, u32[]{:S(2)}) async-start(f32[32,640,160]{1,2,0:T(8,128)} %stack.2), calls=%async_computation.2 | async-start | bytes 26214400 | tf_op jit(solution)/shard_map/all_to_all | solution.py:134
  255.7 309.7 %all-to-all-done.2 = f32[32,640,160]{1,2,0:T(8,128)} async-done(((f32[32,640,160]{1,2,0:T(8,128)}), f32[32,640,160]{1,2,0:T(8,128)}, u32[]{:S(2)}, u32[]{:S(2)}) %all-to-all-start.2) | async-done | bytes 13107232 | tf_op jit(solution)/shard_map/all_to_all | solution.py:134
  565.4 15.7 %convolution_bitcast_fusion = f32[8,64,640]{2,1,0:T(8,128)S(1)} fusion(f32[64,640,1]{1,0,2:T(8,128)S(1)} %reshape.315, f32[8,640,640]{2,1,0:T(8,128)} %bitcast.49), kind=kOutput, calls=%fused_computation.19 | convolution fusion | flops 2516582400 | bytes 14581760 | tf_op jit(solution)/shard_map/dot_general | solution.py:131
  581.2 22.9 %all_to_all.21 = f32[8,64,640]{2,1,0:T(8,128)S(1)} all-to-all(f32[8,64,640]{2,1,0:T(8,128)S(1)} %convolution_bitcast_fusion), channel_id=1, replica_groups=mesh['feature'=4,'kvhead'=8,'seq'=8] {'kvhead'}, dimensions={0} | all-to-all | bytes 2621440 | tf_op jit(solution)/shard_map/all_to_all | solution.py:26
  604.0 0.7 reduce_sum.82
  (54 shorter events, 3.0 us)
Async XLA Ops:
  6.5 82.8 %all-reduce.3.cloned.1.call-start = ((), (), s32[]{:S(2)}) async-start(), calls=%async_computation.5 | async-start | bytes 139264
  15.7 2.5 copy-start.12
  15.7 4.8 copy-start.11
  19.6 0.6 copy-start.10
  20.3 164.8 %all-gather.4.cloned.1.call-start = ((), (), s32[]{:S(2)}) async-start(), calls=%async_computation.4 | async-start | bytes 9510912 | tf_op jit(solution)/shard_map/all_gather | solution.py:76
  22.4 1.9 copy-start.8
  24.3 1.9 copy-start.7
  90.6 5.3 copy-start.4
  95.9 3.3 copy-start
  99.2 3.5 copy-start.2
  107.1 98.3 %all-to-all-start.1 = ((f32[4,256,1,5]{1,2,3,0:T(1,128)}), f32[4,256,1,5]{1,2,3,0:T(1,128)S(1)}, u32[]{:S(2)}, u32[]{:S(2)}) async-start(f32[4,256,1,5]{1,2,3,0:T(1,128)} %broadcast_in_dim.20), calls=%async_computation.1 | async-start | bytes 40960 | tf_op jit(solution)/shard_map/all_to_all | solution.py:11
  185.1 9.6 %copy-start.6 = (f32[64,5,2064]{2,0,1:T(8,128)S(1)}, f32[64,5,2064]{2,0,1:T(8,128)}, u32[]{:S(2)}) copy-start(f32[64,5,2064]{2,0,1:T(8,128)} %fusion.2) | copy-start | bytes 7925764
  194.7 2.5 copy-start.5
  197.3 2.5 copy-start.1
  199.8 2.7 copy-start.3
  205.7 34.4 %copy-start.9 = (f32[640,160]{0,1:T(8,128)S(1)}, f32[640,160]{0,1:T(8,128)}, u32[]{:S(2)}) copy-start(f32[640,160]{0,1:T(8,128)} %param.10) | copy-start | bytes 1228804
  246.3 319.1 %all-to-all-start.2 = ((f32[32,640,160]{1,2,0:T(8,128)}), f32[32,640,160]{1,2,0:T(8,128)}, u32[]{:S(2)}, u32[]{:S(2)}) async-start(f32[32,640,160]{1,2,0:T(8,128)} %stack.2), calls=%async_computation.2 | async-start | bytes 26214400 | tf_op jit(solution)/shard_map/all_to_all | solution.py:134
Sparse Core Ops, SparseCore 0:
  20.4 68.9 all-reduce.2
  91.1 93.9 all-gather.3
